TPU v7x, 32 devices: a whole 2x2x4 slice. The times are simulated.
32 devices in a mesh: queue: 8 (over z, y), mp: 4 (over x, core).
Axes of the slice: x: 2, y: 2, z: 4, core: 2. Of those that a mesh axis runs over, the one named last changes fastest.
Arguments:
- state: bfloat16 [8, 512, 3072], P('queue', None, 'mp')
- key_cache: bfloat16 [8, 32, 3072], P('queue', None, 'mp'), as said below
- value_cache: bfloat16 [8, 32, 3072], P('queue', None, 'mp'), may hold values from -15 to 15
- level_gain: float32 [50, 3072], P(None, 'mp'), may hold values from 0.25 to 1.75
- sigma: float32 [51], replicated, may hold values from 0.05 to 1.5
- levels: int32 [8], P('queue'), may hold values from 0 to 49
- group_len: int32 [8], replicated, may hold values from 256 to 512, as said below
- ctx_ids: int32 [8, 6], P('queue'), may hold values from 0 to 6, as said below
- ctx_count: int32 [8], P('queue'), may hold values from 0 to 6, as said below
Outputs:
- advanced: bfloat16 [8, 512, 3072], P('queue', None, 'mp')
Inputs may be any that keep to these rules, and one draw needn't show every extreme that they name: `group_len`: some group has exactly 512 live tokens. `ctx_count`: slot c lists at most min(c, 6) blocks, and the last slot lists exactly 6. `ctx_ids`: the first ctx_count[c] entries of slot c are distinct blocks of index below c; the other entries are 0. `key_cache`: keys of the clean context blocks.
All inputs are finite; a program needn't handle non-finite values.
Results may differ from a plain program's by a relative error of at most 0.015.
The roundings to bfloat16 on the way count: a program that leaves them out, or rounds other values in their place, can miss the bound.
Values may be sent and summed in bfloat16 or wider, within the bound.
No kernel may reach another device: no remote copies, remote signals or barrier semaphores. Data moves between devices by JAX's collectives and lax.ppermute only.
A program may use at most 64 MiB of HBM per device.

v0:
```python
import jax
import jax.numpy as jnp
from jax import lax
from jax.sharding import PartitionSpec as P

HEAD_DIM = 128
FEAT = 3072
STEPS = 2


def shifted(array, axis, by):
    peers = lax.axis_size(axis)
    return lax.ppermute(array, axis, [(i, (i + by) % peers) for i in range(peers)])


def absorb(state_carry, queries, all_keys, all_values, key_live):
    running_max, running_sum, weighted = state_carry
    heads_here = running_max.shape[0]
    scaling = HEAD_DIM ** (-0.5)

    def one_head(inputs):
        head_index, max_head, sum_head, weighted_head = inputs
        query_head = lax.dynamic_slice_in_dim(queries, head_index * HEAD_DIM, HEAD_DIM, 1)
        key_head = lax.dynamic_slice_in_dim(all_keys, head_index * HEAD_DIM, HEAD_DIM, 1)
        value_head = lax.dynamic_slice_in_dim(all_values, head_index * HEAD_DIM, HEAD_DIM, 1)
        scores = (
            jnp.einsum("rd,kd->rk", query_head, key_head, preferred_element_type=jnp.float32)
            * scaling
        )
        scores = jnp.where(key_live[None, :], scores, -jnp.inf)
        new_max = jnp.maximum(max_head, jnp.max(scores, axis=1))
        weights = jnp.exp(scores - new_max[:, None])
        factor = jnp.exp(max_head - new_max)
        new_sum = sum_head * factor + jnp.sum(weights, axis=1)
        new_weighted = weighted_head * factor[:, None] + jnp.dot(
            weights.astype(jnp.bfloat16), value_head, preferred_element_type=jnp.float32
        )
        return (new_max, new_sum, new_weighted)

    return lax.map(one_head, (jnp.arange(heads_here), running_max, running_sum, weighted))


def on_device(
    state, key_cache, value_cache, level_gain, sigma, levels, group_len, ctx_ids, ctx_count
):
    row_count = state.shape[1]
    feature_count = state.shape[2]
    block_rows = key_cache.shape[1]
    heads_here = feature_count // HEAD_DIM
    groups = lax.axis_size("queue")
    slot_index = lax.axis_index("queue")
    block_index = jnp.arange(groups)
    sigma_index = jnp.arange(sigma.shape[0])
    level_range = jnp.arange(level_gain.shape[0])
    level_now, ids_now, count_now = (levels, ctx_ids, ctx_count)
    current = state[0]
    for step_index in range(STEPS):
        if step_index > 0:
            level_now, ids_now, count_now = shifted((level_now, ids_now, count_now), "queue", -1)
        level_index = level_now[0]
        level_pick = (level_range == level_index).astype(jnp.float32)
        gain_row = jnp.dot(level_pick[None, :], level_gain, precision=lax.Precision.HIGHEST)
        step_size = jnp.sum(jnp.where(sigma_index == level_index + 1, sigma, 0.0)) - jnp.sum(
            jnp.where(sigma_index == level_index, sigma, 0.0)
        )
        block_list = ids_now[0]
        list_live = jnp.arange(block_list.shape[0]) < count_now[0]
        length = jnp.sum(jnp.where(block_index == slot_index, group_len, 0))
        token_live = jnp.arange(row_count) < length
        widened = current.astype(jnp.float32)
        squares = lax.psum(jnp.sum(widened * widened, axis=1), "mp")
        normed = widened * lax.rsqrt(squares / FEAT + 1e-06)[:, None]
        queries = (normed * gain_row).astype(jnp.bfloat16)
        own_keys = normed.astype(jnp.bfloat16)
        empty_carry = (
            jnp.full((heads_here, row_count), -jnp.inf, jnp.float32),
            jnp.zeros((heads_here, row_count), jnp.float32),
            jnp.zeros((heads_here, row_count, HEAD_DIM), jnp.float32),
        )
        state_carry = absorb(empty_carry, queries, own_keys, current, token_live)
        listed = jnp.any((block_list[:, None] == block_index[None, :]) & list_live[:, None], axis=0)
        key_piece = lax.all_gather(key_cache, "queue", axis=0, tiled=True)
        value_piece = lax.all_gather(value_cache, "queue", axis=0, tiled=True)
        block_count = key_piece.shape[0]
        piece_live = jnp.repeat(listed, block_rows)
        state_carry = absorb(
            state_carry,
            queries,
            key_piece.reshape(block_count * block_rows, feature_count),
            value_piece.reshape(block_count * block_rows, feature_count),
            piece_live,
        )
        running_max, running_sum, weighted = state_carry
        attended = jnp.transpose(weighted / running_sum[:, :, None], (1, 0, 2)).reshape(
            row_count, feature_count
        )
        advanced_rows = jnp.where(token_live[:, None], widened + step_size * attended, widened)
        updated = advanced_rows.astype(jnp.bfloat16)
        current = updated
    current = shifted(current, "queue", STEPS)
    return current[None]


def solution(mesh):
    in_specs = (
        P("queue", None, "mp"),
        P("queue", None, "mp"),
        P("queue", None, "mp"),
        P(None, "mp"),
        P(),
        P("queue"),
        P(),
        P("queue", None),
        P("queue"),
    )
    out_specs = P("queue", None, "mp")
    return jax.shard_map(
        on_device, mesh=mesh, in_specs=in_specs, out_specs=out_specs, check_vma=False
    )
```

profile of v0, /device:TPU:0, one launch (start us, length us, event | category | flops | bytes accessed | tf_op | source)
XLA Modules:
  0.0 237.5 jit_solution(6927961134695069647)
XLA Ops:
  0.0 6.0 %collective-permute-start.1 = (s32[1,6]{1,0:T(1,128)}, s32[1,6]{1,0:T(1,128)S(1)}, u32[]{:S(2)}, u32[]{:S(2)}) collective-permute-start(s32[1,6]{1,0:T(1,128)} %param.24), channel_id=1, source_target_pairs={{0,28},{4,0},{8,4},{12,8},{16,12},{20,16},{24,20},{28,24},{1,29},{... | collective-permute-start | bytes 80 | tf_op jit(solution)/shard_map/ppermute | solution.py:13
  6.5 1.4 collective-permute-start.2
  9.3 1.3 fusion.78
  11.2 33.4 %all_gather.8 = bf16[8,32,768]{2,1,0:T(8,128)(2,1)} all-gather(bf16[1,32,768]{2,1,0:T(8,128)(2,1)} %param.18), channel_id=1, replica_groups=mesh['queue'=8,'mp'=4] {'queue'}, dimensions={0}, use_global_device_ids=true | all-gather | bytes 442368 | tf_op jit(solution)/shard_map/all_gather | solution.py:82
  44.6 31.3 %all_gather.9 = bf16[8,32,768]{2,1,0:T(8,128)(2,1)S(1)} all-gather(bf16[1,32,768]{2,1,0:T(8,128)(2,1)} %param.19), channel_id=1, replica_groups=mesh['queue'=8,'mp'=4] {'queue'}, dimensions={0}, use_global_device_ids=true | all-gather | bytes 442368 | tf_op jit(solution)/shard_map/all_gather | solution.py:83
  75.9 1.4 copy.36
  77.5 5.7 %psum.14 = f32[512]{0:T(512)S(1)} all-reduce(f32[512]{0:T(512)S(1)} %fusion.66), channel_id=1, replica_groups=mesh['queue'=8,'mp'=4] {'mp'}, use_global_device_ids=true, to_apply=%region_4.5 | all-reduce | flops 512 | bytes 4096 | tf_op jit(solution)/shard_map/psum | solution.py:71
  83.6 1.2 copy.37
  84.8 1.3 broadcast.125.clone.2
  86.0 33.6 %while.56 = (s32[]{:T(128)}, f32[6,512]{1,0:T(8,128)S(1)}, f32[6,512]{1,0:T(8,128)S(1)}, f32[6,512,128]{2,1,0:T(8,128)}, s32[6]{0:T(128)S(1)}, /*index=5*/bf16[5...) while((s32[]{:T(128)}, f32[6,512]{1,0:T(8,128)S(1)}, ...), condition=%wide.region_8.9_spmd.clone, body=%wide.region_5.8_spmd.clone.sunk | while | flops 136120320 | bytes 3832019 | solution.py:40
  88.0 1.3 fusion.118
  89.7 1.9 fusion.120
  93.6 1.3 fusion.118
  95.2 2.0 fusion.120
  99.2 1.3 fusion.118
  100.8 2.0 fusion.120
  104.8 1.3 fusion.118
  106.4 2.0 fusion.120
  110.4 1.3 fusion.118
  112.0 2.0 fusion.120
  116.0 1.3 fusion.118
  117.6 2.0 fusion.120
  119.9 24.9 %while.57 = (s32[]{:T(128)}, f32[6,512]{1,0:T(8,128)S(1)}, f32[6,512,128]{1,2,0:T(8,128)S(1)}, f32[6,512]{1,0:T(8,128)S(1)}, f32[6,512]{1,0:T(8,128)S(1)}, /*ind...) while((s32[]{:T(128)}, f32[6,512]{1,0:T(8,128)S(1)}, ...), condition=%wide.region_13.14_spmd.clone, body=%wide.region_10.13_spmd.clone.sunk | while | flops 68159488 | bytes 3447023 | solution.py:40
  121.3 1.2 fusion.123
  122.6 1.2 fusion.126
  125.4 1.2 fusion.123
  126.7 1.2 fusion.126
  129.6 1.2 fusion.123
  130.9 1.2 fusion.126
  133.7 1.2 fusion.123
  135.0 1.2 fusion.126
  137.9 1.2 fusion.123
  139.2 1.2 fusion.126
  142.0 1.2 fusion.123
  143.3 1.2 fusion.126
  146.9 1.2 fusion.82
  150.1 6.6 %psum.15 = f32[512]{0:T(512)S(1)} all-reduce(f32[512]{0:T(512)S(1)} %get-tuple-element.529), channel_id=1, replica_groups=mesh['queue'=8,'mp'=4] {'mp'}, use_global_device_ids=true, to_apply=%region_17.18 | all-reduce | flops 512 | bytes 4096 | tf_op jit(solution)/shard_map/psum | solution.py:71
  156.7 1.1 fusion.62
  157.8 1.2 copy.42
  159.0 1.3 broadcast.125
  160.2 28.3 %while.58 = (s32[]{:T(128)}, f32[6,512]{1,0:T(8,128)S(1)}, f32[6,512]{1,0:T(8,128)S(1)}, f32[6,512,128]{2,1,0:T(8,128)}, s32[6]{0:T(128)S(1)}, /*index=5*/bf16[5...) while((s32[]{:T(128)}, f32[6,512]{1,0:T(8,128)S(1)}, ...), condition=%wide.region_21.22_spmd.clone, body=%wide.region_18.21_spmd.clone.sunk | while | flops 136120320 | bytes 3832019 | solution.py:40
  162.2 1.3 fusion.129
  166.9 1.3 fusion.129
  171.6 1.3 fusion.129
  176.3 1.3 fusion.129
  181.0 1.3 fusion.129
  182.7 1.1 fusion.131
  185.7 1.3 fusion.129
  187.4 1.1 fusion.131
  189.9 25.6 %while.59 = (s32[]{:T(128)}, f32[6,512]{1,0:T(8,128)S(1)}, f32[6,512,128]{1,2,0:T(8,128)S(1)}, f32[6,512]{1,0:T(8,128)S(1)}, f32[6,512]{1,0:T(8,128)S(1)}, /*ind...) while((s32[]{:T(128)}, f32[6,512]{1,0:T(8,128)S(1)}, ...), condition=%wide.region_26.27_spmd.clone, body=%wide.region_23.26_spmd.clone.sunk | while | flops 68159488 | bytes 3447023 | solution.py:40
  191.4 1.2 fusion.134
  192.6 1.3 fusion.137
  195.6 1.2 fusion.134
  196.9 1.3 fusion.137
  199.9 1.2 fusion.134
  201.2 1.3 fusion.137
  204.2 1.2 fusion.134
  205.4 1.3 fusion.137
  208.4 1.2 fusion.134
  209.7 1.3 fusion.137
  212.7 1.2 fusion.134
  214.0 1.3 fusion.137
  216.1 20.2 %collective-permute-done.3 = bf16[512,768]{0,1:T(8,128)(2,1)S(1)} collective-permute-done((bf16[512,768]{0,1:T(8,128)(2,1)S(1)}, bf16[512,768]{0,1:T(8,128)(2,1)S(1)}, u32[]{:S(2)}, u32[]{:S(2)}) %collective-permute-start.3) | collective-permute-done | bytes 786464 | tf_op jit(solution)/shard_map/ppermute | solution.py:13
  236.3 1.2 copy.47
  (248 shorter events, 42.0 us)
Async XLA Ops:
  0.0 83.2 %copy-start = (f32[50,768]{1,0:T(8,128)S(1)}, f32[50,768]{1,0:T(8,128)}, u32[]{:S(2)}) copy-start(f32[50,768]{1,0:T(8,128)} %param.20) | copy-start | bytes 460804
  0.0 189.6 %collective-permute-start.1 = (s32[1,6]{1,0:T(1,128)}, s32[1,6]{1,0:T(1,128)S(1)}, u32[]{:S(2)}, u32[]{:S(2)}) collective-permute-start(s32[1,6]{1,0:T(1,128)} %param.24), channel_id=1, source_target_pairs={{0,28},{4,0},{8,4},{12,8},{16,12},{20,16},{24,20},{28,24},{1,29},{... | collective-permute-start | bytes 80 | tf_op jit(solution)/shard_map/ppermute | solution.py:13
  6.0 138.8 %collective-permute-start = (s32[1]{0:T(128)}, s32[1]{0:T(128)}, u32[]{:S(2)}, u32[]{:S(2)}) collective-permute-start(s32[1]{0:T(128)} %param.22), channel_id=1, source_target_pairs={{0,28},{4,0},{8,4},{12,8},{16,12},{20,16},{24,20},{28,24},{1,29},{... | collective-permute-start | bytes 20 | tf_op jit(solution)/shard_map/ppermute | solution.py:13
  6.5 139.7 %collective-permute-start.2 = (s32[1]{0:T(128)}, s32[1]{0:T(128)}, u32[]{:S(2)}, u32[]{:S(2)}) collective-permute-start(s32[1]{0:T(128)} %param.25), channel_id=1, source_target_pairs={{0,28},{4,0},{8,4},{12,8},{16,12},{20,16},{24,20},{28,24},{1,29},{... | collective-permute-start | bytes 20 | tf_op jit(solution)/shard_map/ppermute | solution.py:13
  86.0 33.6 %copy-start.3 = (s32[1,6]{1,0:T(1,128)S(1)}, s32[1,6]{1,0:T(1,128)}, u32[]{:S(2)}) copy-start(s32[1,6]{1,0:T(1,128)} %param.24) | copy-start | bytes 76
  119.9 27.0 %copy-start.2 = (f32[51]{0:T(128)S(1)}, f32[51]{0:T(128)}, u32[]{:S(2)}) copy-start(f32[51]{0:T(128)} %param.21) | copy-start | bytes 616
  144.8 4.8 %copy-start.1 = (bf16[256,768]{1,0:T(8,128)(2,1)}, bf16[256,768]{1,0:T(8,128)(2,1)S(1)}, u32[]{:S(2)}) copy-start(bf16[256,768]{1,0:T(8,128)(2,1)S(1)} %get-tuple-element.980) | copy-start | bytes 1179652
  216.0 20.3 %collective-permute-start.3 = (bf16[512,768]{0,1:T(8,128)(2,1)S(1)}, bf16[512,768]{0,1:T(8,128)(2,1)S(1)}, u32[]{:S(2)}, u32[]{:S(2)}) collective-permute-start(bf16[512,768]{0,1:T(8,128)(2,1)S(1)} %fusion.69), channel_id=1, source_target_pairs={{0,8},{4,12},{8,16},{12,20},{16,24},{20,28},{24,0},{28,4},{1,9},{5... | collective-permute-start | bytes 2359304 | tf_op jit(solution)/shard_map/ppermute | solution.py:13
where the time goes:
time: 239 us; the launch traced here: 237 us
  blocking collectives  76.9 us (32%)
  matrix products  63.6 us (27%)
  local copies, waits for them, and re-layouts  28.8 us (12%)
  waiting for transfers between devices  20.2 us (8%)
  other arithmetic  18.5 us (8%)
  loops' own time  16.9 us (7%)
  starting transfers between devices  8 us (3%)
  between operations  4.54 us (2%)
    all_gather x1, blocking collectives, on_device(): key_piece = lax.all_gather(key_cache, 'queue', axis=0, tiled=True)  33.4 us
    dot_general x24, matrix products, one_head(): jnp.dot(weights.astype(jnp.bfloat16), value_head, preferred_element_type=...  33.2 us
    all_gather x1, blocking collectives, on_device(): value_piece = lax.all_gather(value_cache, 'queue', axis=0, tiled=True)  31.3 us
    dot_general x24, matrix products, one_head(): jnp.einsum('rd,kd->rk', query_head, key_head, preferred_element_type=jnp....  29.5 us
    ppermute x4, waiting for transfers between devices, shifted(): lax.ppermute(array, axis, [(i, (i + by) % peers) for i in range(peers)])  20.2 us
    another operation x4, loops' own time, absorb(): lax.map(one_head, (jnp.arange(heads_here), running_max, running_sum, weig...  16.9 us
    dynamic_slice x36, local copies, waits for them, and re-layouts, absorb(): lax.map(one_head, (jnp.arange(heads_here), running_max, running_sum, weig...  15 us
    psum x2, blocking collectives, on_device(): squares = lax.psum(jnp.sum(widened * widened, axis=1), 'mp')  12.3 us
  transfers between devices with their start and end apart: 4, of which 1 were waited for; matrix products, arithmetic and copies ran while one was open for 37% of the time, Pallas kernels for 0%

commit v1 on v0

--- a/solution.py
+++ b/solution.py
@@ -6,6 +6,23 @@
 HEAD_DIM = 128
 FEAT = 3072
 STEPS = 2
+
+
+def joined_along(blocks, dim):
+    blocks = jnp.moveaxis(blocks, 0, dim)
+    dims = blocks.shape
+    return blocks.reshape(*dims[:dim], dims[dim] * dims[dim + 1], *dims[dim + 2 :])
+
+
+def collected_by_bits(shard, axis):
+    size, place = (lax.axis_size(axis), lax.axis_index(axis))
+    blocks, bit = (shard[None], 1)
+    while bit < size:
+        other = lax.ppermute(blocks, axis, [(i, i ^ bit) for i in range(size)])
+        low = place & bit == 0
+        blocks = jnp.concatenate([jnp.where(low, blocks, other), jnp.where(low, other, blocks)])
+        bit *= 2
+    return blocks
 
 
 def shifted(array, axis, by):
@@ -79,7 +96,7 @@
         )
         state_carry = absorb(empty_carry, queries, own_keys, current, token_live)
         listed = jnp.any((block_list[:, None] == block_index[None, :]) & list_live[:, None], axis=0)
-        key_piece = lax.all_gather(key_cache, "queue", axis=0, tiled=True)
+        key_piece = joined_along(collected_by_bits(key_cache, "queue"), 0)
         value_piece = lax.all_gather(value_cache, "queue", axis=0, tiled=True)
         block_count = key_piece.shape[0]
         piece_live = jnp.repeat(listed, block_rows)

time: 239 us -> 219 us (0.916)
  blocking collectives: 76.9 us -> 43.6 us
  waiting for transfers between devices: 20.2 us -> 33.8 us
    all_gather x1 -> x0, blocking collectives: 33.4 us -> none  [on_device(): key_piece = lax.all_gather(key_cache, 'queue', axis=0, tiled=True)]
    ppermute x0 -> x3, waiting for transfers between devices: none -> 13.6 us  [collected_by_bits(): other = lax.ppermute(blocks, axis, [(i, i ^ bit) for i in range(size)])]
  transfers between devices with their start and end apart: 4 -> 7, of which waited for: 1 -> 3; matrix products, arithmetic and copies ran while one was open for 37% -> 17% of each run, Pallas kernels for 0% -> 0%
where the time goes in v1:
time: 219 us; the launch traced here: 218 us
  matrix products  63.6 us (29%)
  blocking collectives  43.6 us (20%)
  waiting for transfers between devices  33.8 us (15%)
  local copies, waits for them, and re-layouts  28.5 us (13%)
  other arithmetic  19.4 us (9%)
  loops' own time  15.6 us (7%)
  starting transfers between devices  8.77 us (4%)
  between operations  4.46 us (2%)
    dot_general x24, matrix products, one_head(): jnp.dot(weights.astype(jnp.bfloat16), value_head, preferred_element_type=...  33.2 us
    all_gather x1, blocking collectives, on_device(): value_piece = lax.all_gather(value_cache, 'queue', axis=0, tiled=True)  31.4 us
    dot_general x24, matrix products, one_head(): jnp.einsum('rd,kd->rk', query_head, key_head, preferred_element_type=jnp....  29.5 us
    ppermute x4, waiting for transfers between devices, shifted(): lax.ppermute(array, axis, [(i, (i + by) % peers) for i in range(peers)])  20.2 us
    another operation x4, loops' own time, absorb(): lax.map(one_head, (jnp.arange(heads_here), running_max, running_sum, weig...  15.6 us
    dynamic_slice x36, local copies, waits for them, and re-layouts, absorb(): lax.map(one_head, (jnp.arange(heads_here), running_max, running_sum, weig...  14.1 us
    ppermute x3, waiting for transfers between devices, collected_by_bits(): other = lax.ppermute(blocks, axis, [(i, i ^ bit) for i in range(size)])  13.6 us
    psum x2, blocking collectives, on_device(): squares = lax.psum(jnp.sum(widened * widened, axis=1), 'mp')  12.2 us
  transfers between devices with their start and end apart: 7, of which 3 were waited for; matrix products, arithmetic and copies ran while one was open for 17% of the time, Pallas kernels for 0%

profile of v1, /device:TPU:0, one launch (start us, length us, event | category | flops | bytes accessed | tf_op | source)
XLA Modules:
  0.0 217.7 jit_solution(9713797245042593530)
XLA Ops:
  0.0 6.0 %collective-permute-start.4 = (s32[1,6]{1,0:T(1,128)}, s32[1,6]{1,0:T(1,128)S(1)}, u32[]{:S(2)}, u32[]{:S(2)}) collective-permute-start(s32[1,6]{1,0:T(1,128)} %param.24), channel_id=1, source_target_pairs={{0,28},{4,0},{8,4},{12,8},{16,12},{20,16},{24,20},{28,24},{1,29},{... | collective-permute-start | bytes 80 | tf_op jit(solution)/shard_map/ppermute | solution.py:30
  6.5 1.4 collective-permute-start.5
  9.9 1.3 fusion.78
  11.8 31.4 %all_gather.4 = bf16[8,32,768]{2,1,0:T(8,128)(2,1)S(1)} all-gather(bf16[1,32,768]{2,1,0:T(8,128)(2,1)} %param.19), channel_id=1, replica_groups=mesh['queue'=8,'mp'=4] {'queue'}, dimensions={0}, use_global_device_ids=true | all-gather | bytes 442368 | tf_op jit(solution)/shard_map/all_gather | solution.py:100
  43.2 1.4 copy.36
  44.8 5.7 %psum.14 = f32[512]{0:T(512)S(1)} all-reduce(f32[512]{0:T(512)S(1)} %fusion.66), channel_id=1, replica_groups=mesh['queue'=8,'mp'=4] {'mp'}, use_global_device_ids=true, to_apply=%region_4.5 | all-reduce | flops 512 | bytes 4096 | tf_op jit(solution)/shard_map/psum | solution.py:88
  50.9 1.2 copy.37
  52.1 1.3 broadcast.125.clone.2
  53.3 32.3 %while.56 = (s32[]{:T(128)}, f32[6,512]{1,0:T(8,128)S(1)}, f32[6,512]{1,0:T(8,128)S(1)}, f32[6,512,128]{2,1,0:T(8,128)}, s32[6]{0:T(128)S(1)}, /*index=5*/bf16[5...) while((s32[]{:T(128)}, f32[6,512]{1,0:T(8,128)S(1)}, ...), condition=%wide.region_8.9_spmd.clone, body=%wide.region_5.8_spmd.clone.sunk | while | flops 136120320 | bytes 3832019 | solution.py:57
  55.1 1.3 fusion.118
  56.8 1.9 fusion.120
  60.5 1.3 fusion.118
  62.1 2.0 fusion.120
  65.9 1.3 fusion.118
  67.5 2.0 fusion.120
  71.3 1.3 fusion.118
  72.9 2.0 fusion.120
  76.7 1.3 fusion.118
  78.3 2.0 fusion.120
  82.1 1.3 fusion.118
  83.7 2.0 fusion.120
  86.4 1.2 fusion.82
  90.8 3.8 %collective-permute-done.1 = bf16[2,1,32,768]{3,2,1,0:T(8,128)(2,1)S(1)} collective-permute-done((bf16[2,1,32,768]{3,2,1,0:T(8,128)(2,1)S(1)}, bf16[2,1,32,768]{3,2,1,0:T(8,128)(2,1)S(1)}, u32[]{:S(2)}, u32[]{:S(2)}) %collective-permute-start.1) | collective-permute-done | bytes 98336 | tf_op jit(solution)/shard_map/ppermute | solution.py:21
  95.6 9.8 %collective-permute-done.2 = bf16[4,1,32,768]{3,2,1,0:T(8,128)(2,1)S(1)} collective-permute-done((bf16[4,1,32,768]{3,2,1,0:T(8,128)(2,1)S(1)}, bf16[4,1,32,768]{3,2,1,0:T(8,128)(2,1)S(1)}, u32[]{:S(2)}, u32[]{:S(2)}) %collective-permute-start.2) | collective-permute-done | bytes 196640 | tf_op jit(solution)/shard_map/ppermute | solution.py:21
  106.4 24.9 %while.57 = (s32[]{:T(128)}, f32[6,512]{1,0:T(8,128)S(1)}, f32[6,512,128]{1,2,0:T(8,128)S(1)}, f32[6,512]{1,0:T(8,128)S(1)}, f32[6,512]{1,0:T(8,128)S(1)}, /*ind...) while((s32[]{:T(128)}, f32[6,512]{1,0:T(8,128)S(1)}, ...), condition=%wide.region_13.14_spmd.clone, body=%wide.region_10.13_spmd.clone.sunk | while | flops 68159488 | bytes 3447023 | solution.py:57
  107.8 1.2 fusion.123
  109.1 1.2 fusion.126
  111.9 1.2 fusion.123
  113.2 1.2 fusion.126
  116.1 1.2 fusion.123
  117.4 1.2 fusion.126
  120.2 1.2 fusion.123
  121.5 1.2 fusion.126
  124.4 1.2 fusion.123
  125.7 1.2 fusion.126
  128.5 1.2 fusion.123
  129.8 1.2 fusion.126
  132.5 6.6 %psum.15 = f32[512]{0:T(512)S(1)} all-reduce(f32[512]{0:T(512)S(1)} %get-tuple-element.529), channel_id=1, replica_groups=mesh['queue'=8,'mp'=4] {'mp'}, use_global_device_ids=true, to_apply=%region_17.18 | all-reduce | flops 512 | bytes 4096 | tf_op jit(solution)/shard_map/psum | solution.py:88
  139.1 1.1 fusion.62
  140.2 1.2 copy.42
  141.4 1.3 broadcast.125
  142.6 27.4 %while.58 = (s32[]{:T(128)}, f32[6,512]{1,0:T(8,128)S(1)}, f32[6,512]{1,0:T(8,128)S(1)}, f32[6,512,128]{2,1,0:T(8,128)}, s32[6]{0:T(128)S(1)}, /*index=5*/bf16[5...) while((s32[]{:T(128)}, f32[6,512]{1,0:T(8,128)S(1)}, ...), condition=%wide.region_21.22_spmd.clone, body=%wide.region_18.21_spmd.clone.sunk | while | flops 136120320 | bytes 3832019 | solution.py:57
  144.4 1.3 fusion.129
  149.0 1.3 fusion.129
  153.5 1.3 fusion.129
  158.1 1.3 fusion.129
  162.6 1.3 fusion.129
  164.4 1.1 fusion.131
  167.2 1.3 fusion.129
  170.2 25.6 %while.59 = (s32[]{:T(128)}, f32[6,512]{1,0:T(8,128)S(1)}, f32[6,512,128]{1,2,0:T(8,128)S(1)}, f32[6,512]{1,0:T(8,128)S(1)}, f32[6,512]{1,0:T(8,128)S(1)}, /*ind...) while((s32[]{:T(128)}, f32[6,512]{1,0:T(8,128)S(1)}, ...), condition=%wide.region_26.27_spmd.clone, body=%wide.region_23.26_spmd.clone.sunk | while | flops 68159488 | bytes 3447023 | solution.py:57
  171.6 1.2 fusion.134
  172.9 1.3 fusion.137
  175.9 1.2 fusion.134
  177.2 1.3 fusion.137
  180.1 1.2 fusion.134
  181.4 1.3 fusion.137
  184.4 1.2 fusion.134
  185.7 1.3 fusion.137
  188.7 1.2 fusion.134
  189.9 1.3 fusion.137
  192.9 1.2 fusion.134
  194.2 1.3 fusion.137
  196.4 20.2 %collective-permute-done.6 = bf16[512,768]{0,1:T(8,128)(2,1)S(1)} collective-permute-done((bf16[512,768]{0,1:T(8,128)(2,1)S(1)}, bf16[512,768]{0,1:T(8,128)(2,1)S(1)}, u32[]{:S(2)}, u32[]{:S(2)}) %collective-permute-start.6) | collective-permute-done | bytes 786464 | tf_op jit(solution)/shard_map/ppermute | solution.py:30
  216.5 1.2 copy.47
  (261 shorter events, 44.3 us)
Async XLA Ops:
  0.0 50.5 %copy-start = (f32[50,768]{1,0:T(8,128)S(1)}, f32[50,768]{1,0:T(8,128)}, u32[]{:S(2)}) copy-start(f32[50,768]{1,0:T(8,128)} %param.20) | copy-start | bytes 460804
  0.0 95.5 %collective-permute-start.4 = (s32[1,6]{1,0:T(1,128)}, s32[1,6]{1,0:T(1,128)S(1)}, u32[]{:S(2)}, u32[]{:S(2)}) collective-permute-start(s32[1,6]{1,0:T(1,128)} %param.24), channel_id=1, source_target_pairs={{0,28},{4,0},{8,4},{12,8},{16,12},{20,16},{24,20},{28,24},{1,29},{... | collective-permute-start | bytes 80 | tf_op jit(solution)/shard_map/ppermute | solution.py:30
  6.0 79.7 %collective-permute-start.3 = (s32[1]{0:T(128)}, s32[1]{0:T(128)}, u32[]{:S(2)}, u32[]{:S(2)}) collective-permute-start(s32[1]{0:T(128)} %param.22), channel_id=1, source_target_pairs={{0,28},{4,0},{8,4},{12,8},{16,12},{20,16},{24,20},{28,24},{1,29},{... | collective-permute-start | bytes 20 | tf_op jit(solution)/shard_map/ppermute | solution.py:30
  6.5 88.3 %collective-permute-start.5 = (s32[1]{0:T(128)}, s32[1]{0:T(128)}, u32[]{:S(2)}, u32[]{:S(2)}) collective-permute-start(s32[1]{0:T(128)} %param.25), channel_id=1, source_target_pairs={{0,28},{4,0},{8,4},{12,8},{16,12},{20,16},{24,20},{28,24},{1,29},{... | collective-permute-start | bytes 20 | tf_op jit(solution)/shard_map/ppermute | solution.py:30
  7.9 82.0 %collective-permute-start = (bf16[1,1,32,768]{3,2,1,0:T(8,128)(2,1)}, bf16[1,1,32,768]{3,2,1,0:T(8,128)(2,1)S(1)}, u32[]{:S(2)}, u32[]{:S(2)}) collective-permute-start(bf16[1,1,32,768]{3,2,1,0:T(8,128)(2,1)} %bitcast.129), channel_id=1, source_target_pairs={{0,4},{4,0},{8,12},{12,8},{16,20},{20,16},{24,28},{28,24},{1,5},{5... | collective-permute-start | bytes 147464 | tf_op jit(solution)/shard_map/ppermute | solution.py:21
  53.3 32.3 %copy-start.4 = (s32[1,6]{1,0:T(1,128)S(1)}, s32[1,6]{1,0:T(1,128)}, u32[]{:S(2)}) copy-start(s32[1,6]{1,0:T(1,128)} %param.24) | copy-start | bytes 76
  53.3 33.0 %copy-start.3 = (f32[51]{0:T(128)S(1)}, f32[51]{0:T(128)}, u32[]{:S(2)}) copy-start(f32[51]{0:T(128)} %param.21) | copy-start | bytes 616
  53.3 36.6 %copy-start.2 = (bf16[1,32,768]{2,1,0:T(8,128)(2,1)S(1)}, bf16[1,32,768]{2,1,0:T(8,128)(2,1)}, u32[]{:S(2)}) copy-start(bf16[1,32,768]{2,1,0:T(8,128)(2,1)} %param.18) | copy-start | bytes 147460
  90.0 4.7 %collective-permute-start.1 = (bf16[2,1,32,768]{3,2,1,0:T(8,128)(2,1)S(1)}, bf16[2,1,32,768]{3,2,1,0:T(8,128)(2,1)S(1)}, u32[]{:S(2)}, u32[]{:S(2)}) collective-permute-start(bf16[2,1,32,768]{3,2,1,0:T(8,128)(2,1)S(1)} %pad_maximum_fusion.2), channel_id=1, source_target_pairs={{0,8},{4,12},{8,0},{12,4},{16,24},{20,28},{24,16},{28,20},{1,9},{5... | collective-permute-start | bytes 294920 | tf_op jit(solution)/shard_map/ppermute | solution.py:21
  94.7 10.7 %collective-permute-start.2 = (bf16[4,1,32,768]{3,2,1,0:T(8,128)(2,1)S(1)}, bf16[4,1,32,768]{3,2,1,0:T(8,128)(2,1)S(1)}, u32[]{:S(2)}, u32[]{:S(2)}) collective-permute-start(bf16[4,1,32,768]{3,2,1,0:T(8,128)(2,1)S(1)} %pad_maximum_fusion.1), channel_id=1, source_target_pairs={{0,16},{4,20},{8,24},{12,28},{16,0},{20,4},{24,8},{28,12},{1,17},{... | collective-permute-start | bytes 589832 | tf_op jit(solution)/shard_map/ppermute | solution.py:21
  131.3 0.8 copy-start.1
  196.3 20.2 %collective-permute-start.6 = (bf16[512,768]{0,1:T(8,128)(2,1)S(1)}, bf16[512,768]{0,1:T(8,128)(2,1)S(1)}, u32[]{:S(2)}, u32[]{:S(2)}) collective-permute-start(bf16[512,768]{0,1:T(8,128)(2,1)S(1)} %fusion.69), channel_id=1, source_target_pairs={{0,8},{4,12},{8,16},{12,20},{16,24},{20,28},{24,0},{28,4},{1,9},{5... | collective-permute-start | bytes 2359304 | tf_op jit(solution)/shard_map/ppermute | solution.py:30
